TPU v7x, 512 devices: a whole 4x4x16 slice. The times are simulated.
512 devices in a mesh: row: 32 (over z, core), col: 16 (over y, x).
Axes of the slice: x: 4, y: 4, z: 16, core: 2. Of those that a mesh axis runs over, the one named last changes fastest.
Arguments:
- train_points: float32 [64, 32768], P(None, ('row', 'col')), may hold values from -6 to 6
- cand_points: float32 [64, 32768], P(None, ('row', 'col')), may hold values from -6 to 6
- inv_length: float32 [64], replicated, may hold values from 0.04 to 0.7
- noise: float32 [32768], P(('row', 'col')), may hold values from 0.5 to 4
- targets: float32 [16, 32768], P(None, ('row', 'col')), may hold values from -15 to 15
Outputs:
- solution: float32 [16, 32768], P(None, ('row', 'col'))
- post_mean: float32 [16, 32768], P(None, ('row', 'col'))
All inputs are finite; a program needn't handle non-finite values.
Results may differ from a plain program's by a relative error of at most 0.0047.
Values may be sent and summed in bfloat16 or wider, within the bound.
No kernel may reach another device: no remote copies, remote signals or barrier semaphores. Data moves between devices by JAX's collectives and lax.ppermute only.
A program may use at most 64 MiB of HBM per device.

v0:
```python
import math
import jax
import jax.numpy as jnp
from jax import lax
from jax.sharding import PartitionSpec as P

ITERS = 2
root_five = math.sqrt(5.0)


def matern(left, left_norm, right, right_norm):
    inner = lax.dot_general(
        left, right, (((0,), (0,)), ((), ())), preferred_element_type=jnp.float32
    )
    dist_sq = jnp.maximum(left_norm[:, None] + right_norm[None, :] - 2.0 * inner, 0.0)
    radius = jnp.sqrt(dist_sq)
    return (1.0 + root_five * radius + 5.0 / 3.0 * dist_sq) * jnp.exp(-root_five * radius)


def tile_rows(amount):
    best = 1
    for candidate in range(1, 513):
        if amount % candidate == 0:
            best = candidate
    return best


def accumulate(carried, vector_piece, piece_points, piece_norms, other, other_norms):
    amount = vector_piece.shape[1]
    block = tile_rows(amount)

    def advance(block_index, running):
        offset = block_index * block
        sub_points = lax.dynamic_slice_in_dim(piece_points, offset, block, 1)
        sub_norms = lax.dynamic_slice_in_dim(piece_norms, offset, block, 0)
        sub_vector = lax.dynamic_slice_in_dim(vector_piece, offset, block, 1)
        kernel_tile = matern(sub_points, sub_norms, other, other_norms)
        return running + jnp.dot(
            sub_vector,
            kernel_tile,
            precision=lax.Precision.HIGHEST,
            preferred_element_type=jnp.float32,
        )

    return lax.fori_loop(0, amount // block, advance, carried)


def per_device(train_points, cand_points, inv_length, noise, targets):
    scaled_train = (train_points * inv_length[:, None]).astype(jnp.bfloat16)
    scaled_cand = (cand_points * inv_length[:, None]).astype(jnp.bfloat16)
    row_train, row_cand = (
        lax.all_gather(scaled_train, "col", axis=1, tiled=True),
        lax.all_gather(scaled_cand, "col", axis=1, tiled=True),
    )
    col_train = lax.all_gather(scaled_train, "row", axis=1, tiled=True)
    row_norms = jnp.sum(jnp.square(row_train.astype(jnp.float32)), axis=0)
    cand_norms = jnp.sum(jnp.square(row_cand.astype(jnp.float32)), axis=0)
    col_norms = jnp.sum(jnp.square(col_train.astype(jnp.float32)), axis=0)
    outputs = targets.shape[0]

    def from_columns(other, other_norms, carried, vector_piece):
        return accumulate(carried, vector_piece, col_train, col_norms, other, other_norms)

    def squares(residual):
        return lax.psum(jnp.sum(residual * residual, axis=1), ("row", "col"))

    solution = jnp.zeros_like(targets)
    residual = targets
    direction = targets
    norm_now = squares(residual)
    for iteration in range(ITERS):
        start_total = jnp.zeros((outputs, row_train.shape[1]), jnp.float32)
        partial_image = from_columns(
            row_train, row_norms, start_total, lax.all_gather(direction, "row", axis=1, tiled=True)
        )
        own_image = lax.psum_scatter(partial_image, "col", scatter_dimension=1, tiled=True)
        image = own_image + noise[None, :] * direction
        alpha = norm_now / lax.psum(jnp.sum(direction * image, axis=1), ("row", "col"))
        solution = solution + alpha[:, None] * direction
        residual = residual - alpha[:, None] * image
        norm_next = squares(residual)
        direction = residual + (norm_next / norm_now)[:, None] * direction
        norm_now = norm_next
    mean_start = jnp.zeros((outputs, row_cand.shape[1]), jnp.float32)
    partial_mean = from_columns(
        row_cand, cand_norms, mean_start, lax.all_gather(solution, "row", axis=1, tiled=True)
    )
    post_mean = lax.psum_scatter(partial_mean, "col", scatter_dimension=1, tiled=True)
    return (solution, post_mean)


def solution(mesh):
    placed = (
        P(None, ("row", "col")),
        P(None, ("row", "col")),
        P(),
        P(("row", "col")),
        P(None, ("row", "col")),
    )
    return jax.shard_map(
        per_device,
        mesh=mesh,
        in_specs=placed,
        out_specs=(P(None, ("row", "col")), P(None, ("row", "col"))),
        check_vma=False,
    )
```

profile of v0, /device:TPU:2, one launch (start us, length us, event | category | flops | bytes accessed | tf_op | source)
XLA Modules:
  0.0 763.7 jit_solution(8951887657408759057)
XLA Ops:
  7.2 0.8 copy.22
  8.1 0.8 copy.29
  8.9 0.7 multiply_convert_fusion
  9.6 37.6 %all_gather.19 = bf16[64,2048]{0,1:T(8,128)(2,1)S(1)} all-gather(bf16[64,64]{0,1:T(8,128)(2,1)S(1)} %get-tuple-element.538), channel_id=1, replica_groups=mesh['row'=32,'col'=16] {'row'}, dimensions={1}, use_global_device_ids=true | all-gather | bytes 270336 | tf_op jit(solution)/shard_map/all_gather | solution.py:55
  47.2 0.2 copy.23
  47.4 0.3 multiply_reduce_fusion
  47.8 23.8 %all_gather.20 = bf16[64,1024]{0,1:T(8,128)(2,1)S(1)} all-gather(bf16[64,64]{0,1:T(8,128)(2,1)S(1)} %get-tuple-element.538), channel_id=1, replica_groups=mesh['row'=32,'col'=16] {'col'}, dimensions={1}, use_global_device_ids=true | all-gather | bytes 139264 | tf_op jit(solution)/shard_map/all_gather | solution.py:52
  71.5 0.1 copy.24
  71.7 0.2 multiply_reduce_fusion.2
  71.9 27.5 %all-gather = f32[32,64,16]{1,2,0:T(8,128)S(1)} all-gather(f32[1,64,16]{1,2,0:T(8,128)S(1)} %bitcast.37), channel_id=1, replica_groups=mesh['row'=32,'col'=16] {'row'}, dimensions={0}, use_global_device_ids=true | all-gather | bytes 135168 | tf_op jit(solution)/shard_map/all_gather | solution.py:74
  99.4 0.1 copy.21
  99.5 0.1 reshape.16
  99.6 11.9 %while.42 = (s32[]{:T(128)}, f32[16,1024]{1,0:T(8,128)S(1)}, f32[16,2048]{1,0:T(8,128)S(1)}, f32[2048]{0:T(1024)S(1)}, f32[1024]{0:T(1024)S(1)}, /*index=5*/bf16...) while((s32[]{:T(128)}, f32[16,1024]{1,0:T(8,128)S(1)}, ...), condition=%wide.region_5.0_spmd.clone, body=%wide.region_4.0_spmd.clone.sunk | while | flops 173047808 | bytes 4565169 | solution.py:45
  99.7 0.5 fusion.131
  100.1 0.1 dynamic_slice.95
  100.2 2.4 fusion.132
  102.6 0.5 fusion.131
  103.2 2.4 fusion.132
  105.6 0.5 fusion.131
  106.1 2.4 fusion.132
  108.6 0.5 fusion.131
  109.1 2.4 fusion.132
  111.6 1.0 copy.32
  112.6 83.7 %reduce-scatter.10.cloned.1.call-done = f32[64,16]{1,0:T(8,128)} async-done(((f32[1024,16]{1,0:T(8,128)}), f32[64,16]{1,0:T(8,128)}) %reduce-scatter.10.cloned.1.call-update) | async-done | bytes 4112
  196.4 0.8 copy.33
  197.2 0.1 multiply_reduce_fusion.5
  197.3 101.8 %all-reduce = (f32[16]{0:T(128)S(1)}, f32[16]{0:T(128)S(1)}) all-reduce(f32[16]{0:T(128)S(1)} %get-tuple-element.492, f32[16]{0:T(128)S(1)} %get-tuple-element.491), channel_id=1, replica_groups=mesh['row'=32,'col'=16] {'row','col'}, use_global_device_ids=true, to_apply=%region_1.0 | all-reduce | flops 32 | bytes 256 | tf_op jit(solution)/shard_map/psum | solution.py:65
  299.2 0.2 multiply_reduce_fusion.4
  299.3 100.8 %psum.30 = f32[16]{0:T(128)S(1)} all-reduce(f32[16]{0:T(128)S(1)} %multiply_reduce_fusion.4), channel_id=1, replica_groups=mesh['row'=32,'col'=16] {'row','col'}, use_global_device_ids=true, to_apply=%region_10.0 | all-reduce | flops 16 | bytes 128 | tf_op jit(solution)/shard_map/psum | solution.py:65
  400.3 28.5 %all-gather.1 = f32[32,64,16]{1,2,0:T(8,128)S(1)} all-gather(f32[1,64,16]{1,2,0:T(8,128)S(1)} %fusion.105), channel_id=1, replica_groups=mesh['row'=32,'col'=16] {'row'}, dimensions={0}, use_global_device_ids=true | all-gather | bytes 135168 | tf_op jit(solution)/shard_map/all_gather | solution.py:74
  428.8 0.1 copy.25
  428.9 0.1 reshape.18
  429.0 11.9 %while.43 = (s32[]{:T(128)}, f32[16,1024]{1,0:T(8,128)S(1)}, f32[16,2048]{1,0:T(8,128)S(1)}, f32[2048]{0:T(1024)S(1)}, f32[1024]{0:T(1024)S(1)}, /*index=5*/bf16...) while((s32[]{:T(128)}, f32[16,1024]{1,0:T(8,128)S(1)}, ...), condition=%wide.region_12.0_spmd.clone, body=%wide.region_11.0_spmd.clone.sunk | while | flops 173047808 | bytes 4565169 | solution.py:45
  429.0 0.5 fusion.137
  429.5 2.4 fusion.138
  432.0 0.5 fusion.137
  432.5 2.4 fusion.138
  435.0 0.5 fusion.137
  435.5 2.4 fusion.138
  437.9 0.5 fusion.137
  438.5 2.4 fusion.138
  440.9 1.0 copy.34
  442.0 22.1 %all_gather.23 = bf16[64,1024]{0,1:T(8,128)(2,1)S(1)} all-gather(bf16[64,64]{0,1:T(8,128)(2,1)S(1)} %get-tuple-element.537), channel_id=1, replica_groups=mesh['row'=32,'col'=16] {'col'}, dimensions={1}, use_global_device_ids=true | all-gather | bytes 139264 | tf_op jit(solution)/shard_map/all_gather | solution.py:53
  464.1 0.1 copy.31
  464.2 0.2 multiply_reduce_fusion.1
  464.4 60.8 %reduce-scatter.12.cloned.1.call-done = f32[64,16]{1,0:T(8,128)} async-done(((f32[1024,16]{1,0:T(8,128)}), f32[64,16]{1,0:T(8,128)}) %reduce-scatter.12.cloned.1.call-update) | async-done | bytes 4112
  525.2 0.8 copy.35
  526.0 0.2 multiply_reduce_fusion.3
  526.2 102.1 %psum.31 = f32[16]{0:T(128)S(1)} all-reduce(f32[16]{0:T(128)S(1)} %multiply_reduce_fusion.3), channel_id=1, replica_groups=mesh['row'=32,'col'=16] {'row','col'}, use_global_device_ids=true, to_apply=%region_15.0 | all-reduce | flops 16 | bytes 128 | tf_op jit(solution)/shard_map/psum | solution.py:78
  628.4 28.8 %all-gather.2 = f32[32,64,16]{1,2,0:T(8,128)S(1)} all-gather(f32[1,64,16]{1,2,0:T(8,128)S(1)} %bitcast.44), channel_id=1, replica_groups=mesh['row'=32,'col'=16] {'row'}, dimensions={0}, use_global_device_ids=true | all-gather | bytes 135168 | tf_op jit(solution)/shard_map/all_gather | solution.py:86
  657.2 0.1 copy.28
  657.3 0.1 reshape.20
  657.4 11.9 %while.44 = (s32[]{:T(128)}, f32[16,1024]{1,0:T(8,128)S(1)}, f32[16,2048]{1,0:T(8,128)S(1)}, f32[2048]{0:T(1024)S(1)}, f32[1024]{0:T(1024)S(1)}, /*index=5*/bf16...) while((s32[]{:T(128)}, f32[16,1024]{1,0:T(8,128)S(1)}, ...), condition=%wide.region_18.0_spmd.clone, body=%wide.region_17.0_spmd.clone.sunk | while | flops 173047808 | bytes 4565169 | solution.py:45
  657.4 0.5 fusion.143
  658.0 2.4 fusion.144
  660.4 0.5 fusion.143
  660.9 2.4 fusion.144
  663.4 0.5 fusion.143
  663.9 2.4 fusion.144
  666.3 0.5 fusion.143
  666.9 2.4 fusion.144
  669.3 1.0 copy.36
  670.3 85.4 %reduce-scatter.14.cloned.1.call-done = f32[64,16]{1,0:T(8,128)} async-done(((f32[1024,16]{1,0:T(8,128)}), f32[64,16]{1,0:T(8,128)}) %reduce-scatter.14.cloned.1.call-update) | async-done | bytes 4112
  755.7 1.4 copy.37
  (31 shorter events, 1.2 us)
Async XLA Ops:
  7.2 64.7 %copy-start = (f32[16,64]{1,0:T(8,128)S(1)}, f32[16,64]{1,0:T(8,128)}, u32[]{:S(2)}) copy-start(f32[16,64]{1,0:T(8,128)} %param.15) | copy-start | bytes 12292
  7.2 189.2 %reduce-scatter.10.cloned.1.call-start = ((), (), s32[]{:S(2)}) async-start(), calls=%async_computation.3 | async-start | bytes 557056
  99.6 97.6 %copy-start.2 = (f32[64]{0:T(128)S(1)}, f32[64]{0:T(128)}, u32[]{:S(2)}) copy-start(f32[64]{0:T(128)} %param.14) | copy-start | bytes 772
  112.6 412.6 %reduce-scatter.12.cloned.1.call-start = ((), (), s32[]{:S(2)}) async-start(), calls=%async_computation.4 | async-start | bytes 557056
  441.9 313.8 %reduce-scatter.14.cloned.1.call-start = ((), (), s32[]{:S(2)}) async-start(), calls=%async_computation.5 | async-start | bytes 557056
  628.4 29.0 %copy-start.1 = (f32[16,64]{1,0:T(8,128)}, f32[16,64]{1,0:T(8,128)S(1)}, u32[]{:S(2)}) copy-start(f32[16,64]{1,0:T(8,128)S(1)} %multiply_add_fusion) | copy-start | bytes 12292
Sparse Core Ops, SparseCore 0:
  112.7 83.6 reduce-scatter.9
  442.1 83.1 reduce-scatter.11
  670.5 85.2 reduce-scatter.13
where the time goes:
time: 764 us
  blocking collectives  473 us (62%)
  waiting for transfers between devices  230 us (30%)
  matrix products  34.7 us (5%)
  between operations  13.9 us (2%)
  local copies, waits for them, and re-layouts  9.77 us (1%)
    unnamed x6, waiting for transfers between devices  230 us
    psum x2, blocking collectives, squares(): return lax.psum(jnp.sum(residual * residual, axis=1), ('row', 'col'))  203 us
    psum x1, blocking collectives, per_device(): lax.psum(jnp.sum(direction * image, axis=1), ('row', 'col'))  102 us
    all_gather x2, blocking collectives, per_device(): lax.all_gather(direction, 'row', axis=1, tiled=True)  56 us
    all_gather x1, blocking collectives, per_device(): col_train = lax.all_gather(scaled_train, 'row', axis=1, tiled=True)  37.6 us
    dot_general x12, matrix products, advance(): jnp.dot(sub_vector, kernel_tile, precision=lax.Precision.HIGHEST, preferr...  29.1 us
    all_gather x1, blocking collectives, per_device(): lax.all_gather(solution, 'row', axis=1, tiled=True)  28.8 us
    all_gather x1, blocking collectives, per_device(): lax.all_gather(scaled_train, 'col', axis=1, tiled=True)  23.8 us
  transfers between devices with their start and end apart: 3, of which 3 were waited for; matrix products, arithmetic and copies ran while one was open for 0% of the time, Pallas kernels for 0%

commit v1 on v0

--- a/solution.py
+++ b/solution.py
@@ -6,6 +6,11 @@
 
 ITERS = 2
 root_five = math.sqrt(5.0)
+
+
+def exchange_gather(shard, axis, dim):
+    repeated = jnp.stack([shard] * lax.axis_size(axis))
+    return jnp.concatenate(lax.all_to_all(repeated, axis, 0, 0), axis=dim)
 
 
 def matern(left, left_norm, right, right_norm):
@@ -83,7 +88,7 @@
         norm_now = norm_next
     mean_start = jnp.zeros((outputs, row_cand.shape[1]), jnp.float32)
     partial_mean = from_columns(
-        row_cand, cand_norms, mean_start, lax.all_gather(solution, "row", axis=1, tiled=True)
+        row_cand, cand_norms, mean_start, exchange_gather(solution, "row", 1)
     )
     post_mean = lax.psum_scatter(partial_mean, "col", scatter_dimension=1, tiled=True)
     return (solution, post_mean)

time: 764 us -> 774 us (1.013)
  blocking collectives: 473 us -> 446 us
  waiting for transfers between devices: 230 us -> 255 us
  starting transfers between devices: 0.12 us -> 9.07 us
    all_gather x1 -> x0, blocking collectives: 28.8 us -> none  [per_device(): lax.all_gather(solution, 'row', axis=1, tiled=True)]
    unnamed x6, waiting for transfers between devices: 230 us -> 255 us
    all_to_all x0 -> x1, starting transfers between devices: none -> 8.95 us  [exchange_gather(): return jnp.concatenate(lax.all_to_all(repeated, axis, 0, 0), axis=dim)]
  transfers between devices with their start and end apart: 3 -> 4, of which waited for: 3 -> 3; matrix products, arithmetic and copies ran while one was open for 0% -> 0% of each run, Pallas kernels for 0% -> 0%
where the time goes in v1:
time: 774 us; the launch traced here: 773 us
  blocking collectives  446 us (58%)
  waiting for transfers between devices  255 us (33%)
  matrix products  34.7 us (4%)
  between operations  13.9 us (2%)
  local copies, waits for them, and re-layouts  11.3 us (1%)
  starting transfers between devices  9.07 us (1%)
    unnamed x6, waiting for transfers between devices  255 us
    psum x2, blocking collectives, squares(): return lax.psum(jnp.sum(residual * residual, axis=1), ('row', 'col'))  203 us
    psum x1, blocking collectives, per_device(): lax.psum(jnp.sum(direction * image, axis=1), ('row', 'col'))  102 us
    all_gather x2, blocking collectives, per_device(): lax.all_gather(direction, 'row', axis=1, tiled=True)  56.1 us
    all_gather x1, blocking collectives, per_device(): col_train = lax.all_gather(scaled_train, 'row', axis=1, tiled=True)  37.6 us
    dot_general x12, matrix products, advance(): jnp.dot(sub_vector, kernel_tile, precision=lax.Precision.HIGHEST, preferr...  29.1 us
    all_gather x1, blocking collectives, per_device(): lax.all_gather(scaled_cand, 'col', axis=1, tiled=True)  23.8 us
    all_gather x1, blocking collectives, per_device(): lax.all_gather(scaled_train, 'col', axis=1, tiled=True)  23.8 us
  transfers between devices with their start and end apart: 4, of which 3 were waited for; matrix products, arithmetic and copies ran while one was open for 0% of the time, Pallas kernels for 0%

profile of v1, /device:TPU:2, one launch (start us, length us, event | category | flops | bytes accessed | tf_op | source)
XLA Modules:
  0.0 772.8 jit_solution(12190338384079899961)
XLA Ops:
  7.2 0.8 copy.20
  8.1 0.8 copy.27
  8.9 0.7 multiply_convert_fusion
  9.6 37.6 %all_gather.16 = bf16[64,2048]{0,1:T(8,128)(2,1)S(1)} all-gather(bf16[64,64]{0,1:T(8,128)(2,1)S(1)} %get-tuple-element.538), channel_id=1, replica_groups=mesh['row'=32,'col'=16] {'row'}, dimensions={1}, use_global_device_ids=true | all-gather | bytes 270336 | tf_op jit(solution)/shard_map/all_gather | solution.py:60
  47.2 0.2 copy.21
  47.4 0.3 multiply_reduce_fusion
  47.8 23.8 %all_gather.17 = bf16[64,1024]{0,1:T(8,128)(2,1)S(1)} all-gather(bf16[64,64]{0,1:T(8,128)(2,1)S(1)} %get-tuple-element.538), channel_id=1, replica_groups=mesh['row'=32,'col'=16] {'col'}, dimensions={1}, use_global_device_ids=true | all-gather | bytes 139264 | tf_op jit(solution)/shard_map/all_gather | solution.py:57
  71.5 0.1 copy.22
  71.7 0.2 multiply_reduce_fusion.2
  71.9 27.5 %all-gather = f32[32,64,16]{1,2,0:T(8,128)S(1)} all-gather(f32[1,64,16]{1,2,0:T(8,128)S(1)} %bitcast.33), channel_id=1, replica_groups=mesh['row'=32,'col'=16] {'row'}, dimensions={0}, use_global_device_ids=true | all-gather | bytes 135168 | tf_op jit(solution)/shard_map/all_gather | solution.py:79
  99.5 0.1 reshape.26
  99.6 11.9 %while.42 = (s32[]{:T(128)}, f32[16,1024]{1,0:T(8,128)S(1)}, f32[16,2048]{1,0:T(8,128)S(1)}, f32[2048]{0:T(1024)S(1)}, f32[1024]{0:T(1024)S(1)}, /*index=5*/bf16...) while((s32[]{:T(128)}, f32[16,1024]{1,0:T(8,128)S(1)}, ...), condition=%wide.region_5.0_spmd.clone, body=%wide.region_4.0_spmd.clone.sunk | while | flops 173047808 | bytes 4565169 | solution.py:50
  99.7 0.5 fusion.131
  100.2 2.4 fusion.132
  102.6 0.5 fusion.131
  103.2 2.4 fusion.132
  105.6 0.5 fusion.131
  106.1 2.4 fusion.132
  108.6 0.5 fusion.131
  109.1 2.4 fusion.132
  111.5 1.0 copy.30
  112.6 83.7 %reduce-scatter.10.cloned.1.call-done = f32[64,16]{1,0:T(8,128)} async-done(((f32[1024,16]{1,0:T(8,128)}), f32[64,16]{1,0:T(8,128)}) %reduce-scatter.10.cloned.1.call-update) | async-done | bytes 4112
  196.4 0.8 copy.31
  197.2 0.1 multiply_reduce_fusion.5
  197.3 101.8 %all-reduce = (f32[16]{0:T(128)S(1)}, f32[16]{0:T(128)S(1)}) all-reduce(f32[16]{0:T(128)S(1)} %get-tuple-element.492, f32[16]{0:T(128)S(1)} %get-tuple-element.491), channel_id=1, replica_groups=mesh['row'=32,'col'=16] {'row','col'}, use_global_device_ids=true, to_apply=%region_1.0 | all-reduce | flops 32 | bytes 256 | tf_op jit(solution)/shard_map/psum | solution.py:70
  299.1 0.2 multiply_reduce_fusion.4
  299.3 100.8 %psum.30 = f32[16]{0:T(128)S(1)} all-reduce(f32[16]{0:T(128)S(1)} %multiply_reduce_fusion.4), channel_id=1, replica_groups=mesh['row'=32,'col'=16] {'row','col'}, use_global_device_ids=true, to_apply=%region_10.0 | all-reduce | flops 16 | bytes 128 | tf_op jit(solution)/shard_map/psum | solution.py:70
  400.2 28.5 %all-gather.1 = f32[32,64,16]{1,2,0:T(8,128)S(1)} all-gather(f32[1,64,16]{1,2,0:T(8,128)S(1)} %fusion.105), channel_id=1, replica_groups=mesh['row'=32,'col'=16] {'row'}, dimensions={0}, use_global_device_ids=true | all-gather | bytes 135168 | tf_op jit(solution)/shard_map/all_gather | solution.py:79
  428.9 0.1 reshape.28
  429.0 11.9 %while.43 = (s32[]{:T(128)}, f32[16,1024]{1,0:T(8,128)S(1)}, f32[16,2048]{1,0:T(8,128)S(1)}, f32[2048]{0:T(1024)S(1)}, f32[1024]{0:T(1024)S(1)}, /*index=5*/bf16...) while((s32[]{:T(128)}, f32[16,1024]{1,0:T(8,128)S(1)}, ...), condition=%wide.region_12.0_spmd.clone, body=%wide.region_11.0_spmd.clone.sunk | while | flops 173047808 | bytes 4565169 | solution.py:50
  429.0 0.5 fusion.137
  429.5 2.4 fusion.138
  432.0 0.5 fusion.137
  432.5 2.4 fusion.138
  434.9 0.5 fusion.137
  435.5 2.4 fusion.138
  437.9 0.5 fusion.137
  438.5 2.4 fusion.138
  440.9 1.0 copy.32
  441.9 83.3 %reduce-scatter.12.cloned.1.call-done = f32[64,16]{1,0:T(8,128)} async-done(((f32[1024,16]{1,0:T(8,128)}), f32[64,16]{1,0:T(8,128)}) %reduce-scatter.12.cloned.1.call-update) | async-done | bytes 4112
  525.2 0.8 copy.33
  526.0 0.2 multiply_reduce_fusion.3
  526.2 101.8 %psum.31 = f32[16]{0:T(128)S(1)} all-reduce(f32[16]{0:T(128)S(1)} %multiply_reduce_fusion.3), channel_id=1, replica_groups=mesh['row'=32,'col'=16] {'row','col'}, use_global_device_ids=true, to_apply=%region_15.0 | all-reduce | flops 16 | bytes 128 | tf_op jit(solution)/shard_map/psum | solution.py:83
  628.2 0.8 reshape.35
  629.0 8.9 %all-to-all-start = ((f32[32,1,1024]{2,1,0:T(1,128)}), f32[32,1,1024]{2,1,0:T(1,128)S(1)}, u32[]{:S(2)}, u32[]{:S(2)}) async-start(f32[32,1,1024]{2,1,0:T(1,128)} %reshape.35), calls=%async_computation | async-start | bytes 262144 | tf_op jit(solution)/shard_map/all_to_all | solution.py:13
  638.0 23.8 %all_gather.19 = bf16[64,1024]{0,1:T(8,128)(2,1)S(1)} all-gather(bf16[64,64]{0,1:T(8,128)(2,1)S(1)} %get-tuple-element.537), channel_id=1, replica_groups=mesh['row'=32,'col'=16] {'col'}, dimensions={1}, use_global_device_ids=true | all-gather | bytes 139264 | tf_op jit(solution)/shard_map/all_gather | solution.py:58
  661.8 0.1 copy.29
  662.0 0.2 multiply_reduce_fusion.1
  662.2 0.6 broadcast.251
  662.8 1.0 reduce
  663.8 0.1 reshape.36
  664.0 0.1 reshape.24
  664.1 11.9 %while.44 = (s32[]{:T(128)}, f32[16,1024]{1,0:T(8,128)S(1)}, f32[16,2048]{1,0:T(8,128)S(1)}, f32[2048]{0:T(1024)S(1)}, f32[1024]{0:T(1024)S(1)}, /*index=5*/bf16...) while((s32[]{:T(128)}, f32[16,1024]{1,0:T(8,128)S(1)}, ...), condition=%wide.region_18.0_spmd.clone, body=%wide.region_17.0_spmd.clone.sunk | while | flops 173047808 | bytes 4565169 | solution.py:50
  664.1 0.5 fusion.143
  664.7 2.4 fusion.144
  667.1 0.5 fusion.143
  667.7 2.4 fusion.144
  670.1 0.5 fusion.143
  670.6 2.4 fusion.144
  673.1 0.5 fusion.143
  673.6 2.4 fusion.144
  676.0 1.0 copy.34
  677.1 87.8 %reduce-scatter.14.cloned.1.call-done = f32[64,16]{1,0:T(8,128)} async-done(((f32[1024,16]{1,0:T(8,128)}), f32[64,16]{1,0:T(8,128)}) %reduce-scatter.14.cloned.1.call-update) | async-done | bytes 4112
  764.8 1.4 copy.35
  (37 shorter events, 1.6 us)
Async XLA Ops:
  7.2 64.7 %copy-start = (f32[16,64]{1,0:T(8,128)S(1)}, f32[16,64]{1,0:T(8,128)}, u32[]{:S(2)}) copy-start(f32[16,64]{1,0:T(8,128)} %param.15) | copy-start | bytes 12292
  7.2 189.2 %reduce-scatter.10.cloned.1.call-start = ((), (), s32[]{:S(2)}) async-start(), calls=%async_computation.4 | async-start | bytes 557056
  99.6 97.6 %copy-start.2 = (f32[64]{0:T(128)S(1)}, f32[64]{0:T(128)}, u32[]{:S(2)}) copy-start(f32[64]{0:T(128)} %param.14) | copy-start | bytes 772
  112.6 412.6 %reduce-scatter.12.cloned.1.call-start = ((), (), s32[]{:S(2)}) async-start(), calls=%async_computation.5 | async-start | bytes 557056
  628.1 36.0 %copy-start.1 = (f32[16,64]{1,0:T(8,128)}, f32[16,64]{1,0:T(8,128)S(1)}, u32[]{:S(2)}) copy-start(f32[16,64]{1,0:T(8,128)S(1)} %multiply_add_fusion) | copy-start | bytes 12292
  629.0 33.2 %all-to-all-start = ((f32[32,1,1024]{2,1,0:T(1,128)}), f32[32,1,1024]{2,1,0:T(1,128)S(1)}, u32[]{:S(2)}, u32[]{:S(2)}) async-start(f32[32,1,1024]{2,1,0:T(1,128)} %reshape.35), calls=%async_computation | async-start | bytes 262144 | tf_op jit(solution)/shard_map/all_to_all | solution.py:13
  637.9 126.9 %reduce-scatter.14.cloned.1.call-start = ((), (), s32[]{:S(2)}) async-start(), calls=%async_computation.6 | async-start | bytes 557056
Sparse Core Ops, SparseCore 0:
  112.7 83.6 reduce-scatter.9
  442.0 83.1 reduce-scatter.11
  677.2 87.5 reduce-scatter.13
